TPU v7x, 32 devices: a whole 2x2x4 slice. The times are simulated.
32 devices in a mesh: parts: 2 (over y), clip: 4 (over x, core), tensor: 4 (over z).
Axes of the slice: x: 2, y: 2, z: 4, core: 2. Of those that a mesh axis runs over, the one named last changes fastest.
Arguments:
- clips: bfloat16 [32, 128, 4096], P(('parts', 'clip'), None, 'tensor'), parts along dimension 0, may hold values from -6 to 6
- targets: bfloat16 [32, 128, 4096], P(('parts', 'clip'), None, 'tensor'), parts along dimension 0, may hold values from -6 to 6
- lengths: int32 [32], P(('parts', 'clip')), parts along dimension 0, may hold values from 32 to 128, as said below
- gate_weight: bfloat16 [4096, 7168], P(None, 'tensor'), may hold values from -0.09375 to 0.09375
- up_weight: bfloat16 [4096, 7168], P(None, 'tensor'), may hold values from -0.09375 to 0.09375
- down_weight: bfloat16 [7168, 4096], P('tensor'), may hold values from -0.0625 to 0.0625
- proj_in: bfloat16 [64, 7168], P(None, 'tensor'), may hold values from -0.0625 to 0.0625
- proj_out: bfloat16 [64, 4096], replicated, may hold values from -0.09375 to 0.09375
- inv_hessian: bfloat16 [4096, 4096], P('clip', 'tensor'), may hold values from -0.2 to 2.2, as said below
- test_sketches: bfloat16 [4096, 4096], P('clip', 'tensor'), may hold values from -6 to 6
Outputs:
- scores: float32 [32, 4096], P(('parts', 'clip'), 'tensor'), parts along dimension 0
There are 2 independent parts, one for each index of `parts`. A program takes and returns all parts, laid end to end along the dimension named above; an argument that names none is the same for every part. Nothing has to cross between parts.
Inputs may be any that keep to these rules, and one draw needn't show every extreme that they name: `lengths`: every clip has between 32 and 128 valid tokens; in each part one clip has exactly 128 and another exactly 32. `inv_hessian`: the same matrix in both parts.
All inputs are finite; a program needn't handle non-finite values.
Results may differ from a plain program's by a relative error of at most 0.0066.
Values may be sent and summed in bfloat16 or wider, within the bound.
A program may use at most 192 MiB of HBM per device.

v0:
```python
import jax
import jax.numpy as jnp
from jax import lax
from jax.sharding import PartitionSpec as P


def on_device(
    clips,
    targets,
    lengths,
    gate_weight,
    up_weight,
    down_weight,
    proj_in,
    proj_out,
    inv_hessian,
    test_sketches,
):
    clip_count, slot_count, width_part = clips.shape
    row_count = clip_count * slot_count
    proj_size = proj_in.shape[0]
    flat_tokens = clips.reshape(row_count, width_part)
    piece = lax.all_gather(flat_tokens, "tensor", axis=1, tiled=True)
    gate_act = jnp.dot(piece, gate_weight, preferred_element_type=jnp.float32)
    up_act = jnp.dot(piece, up_weight, preferred_element_type=jnp.float32)
    hidden = (jax.nn.silu(gate_act) * up_act).astype(jnp.bfloat16)
    left_part = jnp.dot(hidden, proj_in.T, preferred_element_type=jnp.float32)
    tensor_pos = lax.axis_index("tensor")
    lens_float = lengths.astype(jnp.float32)
    partial_out = jnp.dot(hidden, down_weight, preferred_element_type=jnp.float32)
    outputs = lax.psum_scatter(partial_out, "tensor", scatter_dimension=1, tiled=True)
    position = jnp.arange(slot_count, dtype=jnp.int32)
    masked = (position[None, :] < lengths[:, None]).astype(jnp.float32) / lens_float[:, None]
    golden = targets.reshape(row_count, width_part).astype(jnp.float32)
    differ = jnp.clip(outputs - golden, -1.0, 1.0)
    grad_out = (differ * masked.reshape(row_count)[:, None]).astype(jnp.bfloat16)
    proj_cols = lax.dynamic_slice_in_dim(proj_out, tensor_pos * width_part, width_part, 1)
    right_part = jnp.dot(grad_out, proj_cols.T, preferred_element_type=jnp.float32)
    joined = lax.psum(jnp.concatenate([left_part, right_part], axis=1), "tensor")
    left_full = joined[:, :proj_size].reshape(clip_count, slot_count, proj_size)
    right_full = joined[:, proj_size:].reshape(clip_count, slot_count, proj_size)
    sketch = jnp.einsum("cti,ctk->cik", left_full, right_full, precision=lax.Precision.HIGHEST)
    flat_sketch = sketch.reshape(clip_count, proj_size * proj_size).astype(jnp.bfloat16)
    precond = jnp.dot(
        flat_sketch,
        lax.all_gather(inv_hessian, "clip", axis=0, tiled=True),
        preferred_element_type=jnp.float32,
    ).astype(jnp.bfloat16)
    partial_scores = lax.dot_general(
        precond,
        lax.all_gather(test_sketches, "clip", axis=0, tiled=True),
        (((1,), (1,)), ((), ())),
        preferred_element_type=jnp.float32,
    )
    return lax.psum_scatter(partial_scores, "tensor", scatter_dimension=1, tiled=True)


def solution(mesh):
    in_specs = (
        P(("parts", "clip"), None, "tensor"),
        P(("parts", "clip"), None, "tensor"),
        P(("parts", "clip")),
        P(None, "tensor"),
        P(None, "tensor"),
        P("tensor", None),
        P(None, "tensor"),
        P(),
        P("clip", "tensor"),
        P("clip", "tensor"),
    )
    out_specs = P(("parts", "clip"), "tensor")
    return jax.shard_map(
        on_device, mesh=mesh, in_specs=in_specs, out_specs=out_specs, check_vma=False
    )
```

profile of v0, /device:TPU:0, one launch (start us, length us, event | category | flops | bytes accessed | tf_op | source)
XLA Modules:
  0.0 461.4 jit_solution(14233535387168297329)
XLA Ops:
  7.4 0.0 copy-start
  7.4 0.7 all-gather.4.cloned.1.call-update
  8.1 0.0 reduce-scatter.5.cloned.1.call-start
  8.1 85.1 %all-gather.4.cloned.1.call-done = bf16[512,4096]{1,0:T(8,128)(2,1)} async-done(((bf16[512,1024]{1,0:T(8,128)(2,1)}), bf16[512,4096]{1,0:T(8,128)(2,1)}) %all-gather.4.cloned.1.call-update) | async-done | bytes 4194320 | tf_op jit(solution)/shard_map/all_gather | solution.py:23
  93.3 14.7 %fusion.10 = f32[512,1792]{1,0:T(8,128)} fusion(bf16[512,4096]{1,0:T(8,128)(2,1)} %all-gather.4.cloned.1.call-done, bf16[4096,1792]{1,0:T(8,128)(2,1)} %param.13), kind=kOutput, calls=%fused_computation.20 | convolution fusion | flops 7516192768 | bytes 22544384 | tf_op jit(solution)/shard_map/dot_general | solution.py:24
  107.9 12.8 %multiply_convert_fusion = bf16[512,1792]{1,0:T(8,128)(2,1)S(1)} fusion(f32[512,1792]{1,0:T(8,128)} %fusion.10, bf16[512,4096]{1,0:T(8,128)(2,1)S(1)} %copy-done.3, bf16[4096,1792]{1,0:T(8,128)(2,1)} %param.14), kind=kOutput, calls=%fused_computation.1 | convolution fusion | flops 7521697792 | bytes 24379392 | tf_op jit(solution)/shard_map/dot_general | solution.py:25
  120.8 9.9 %fusion.12 = f32[512,4096]{1,0:T(8,128)} fusion(bf16[512,1792]{1,0:T(8,128)(2,1)S(1)} %multiply_convert_fusion, bf16[1792,4096]{1,0:T(8,128)(2,1)S(1)} %bitcast.34), kind=kOutput, calls=%fused_computation.22 | convolution fusion | flops 7516192768 | bytes 24903680 | tf_op jit(solution)/shard_map/dot_general | solution.py:30
  130.8 0.0 reduce-scatter.5.cloned.1.call-update
  130.8 0.0 all-reduce.2.cloned.1.call-start
  130.9 0.6 copy-done.2
  131.4 0.1 divide_bitcast_fusion
  131.5 1.6 fusion.11
  133.1 140.9 %reduce-scatter.5.cloned.1.call-done = f32[512,1024]{1,0:T(8,128)} async-done(((f32[512,4096]{1,0:T(8,128)}), f32[512,1024]{1,0:T(8,128)}) %reduce-scatter.5.cloned.1.call-update) | async-done | bytes 2097168 | tf_op jit(solution)/shard_map/reduce_scatter | solution.py:31
  274.0 1.9 fusion.2
  275.9 0.4 fusion.7
  276.4 0.7 pad_maximum_fusion
  277.1 0.0 all-reduce.2.cloned.1.call-update
  277.1 0.0 all-gather.6.cloned.1.call-start
  277.2 0.5 all-gather.6.cloned.1.call-update
  277.7 0.0 all-gather.8.cloned.1.call-start
  277.7 0.5 all-gather.8.cloned.1.call-update
  278.3 0.2 reduce-scatter.7.cloned.1.call-start
  278.5 34.8 %all-reduce.2.cloned.1.call-done = f32[512,128]{0,1:T(8,128)} async-done(((f32[512,128]{0,1:T(8,128)}), f32[512,128]{0,1:T(8,128)}) %all-reduce.2.cloned.1.call-update) | async-done | bytes 262160 | tf_op jit(solution)/shard_map/psum | solution.py:39
  313.3 1.0 slice_bitcast_fusion.1
  314.3 0.3 convolution_convert_fusion
  314.6 0.1 convert_element_type.39
  314.7 23.4 %all-gather.6.cloned.1.call-done = bf16[4096,1024]{1,0:T(8,128)(2,1)} async-done(((bf16[1024,1024]{1,0:T(8,128)(2,1)}), bf16[4096,1024]{1,0:T(8,128)(2,1)}) %all-gather.6.cloned.1.call-update) | async-done | bytes 8388624 | tf_op jit(solution)/shard_map/all_gather | solution.py:46
  338.1 59.7 %all-gather.8.cloned.1.call-done = bf16[4096,1024]{1,0:T(8,128)(2,1)} async-done(((bf16[1024,1024]{1,0:T(8,128)(2,1)}), bf16[4096,1024]{1,0:T(8,128)(2,1)}) %all-gather.8.cloned.1.call-update) | async-done | bytes 8388624 | tf_op jit(solution)/shard_map/all_gather | solution.py:51
  397.8 10.6 %convolution_bitcast_fusion = f32[4096,4]{1,0:T(8,128)} fusion(bf16[4096,1024]{1,0:T(8,128)(2,1)} %all-gather.8.cloned.1.call-done, bf16[4,4096]{1,0:T(4,128)(2,1)S(1)} %convert_element_type.39, bf16[4096,1024]{1,0:T(8,128)(2,1)} %all-gather.6.cloned.1.call-done), kind=kOutput, calls=%fused_computation | convolution fusion | flops 67112960 | bytes 16875520
  408.4 0.0 reduce-scatter.7.cloned.1.call-update
  408.4 44.0 %reduce-scatter.7.cloned.1.call-done = f32[1024,4]{1,0:T(8,128)} async-done(((f32[4096,4]{1,0:T(8,128)}), f32[1024,4]{1,0:T(8,128)}) %reduce-scatter.7.cloned.1.call-update) | async-done | bytes 16400
  452.4 1.8 copy.16
  (17 shorter events, 0.0 us)
Async XLA Ops:
  7.4 268.5 %copy-start = (bf16[64,4096]{1,0:T(8,128)(2,1)S(1)}, bf16[64,4096]{1,0:T(8,128)(2,1)}, u32[]{:S(2)}) copy-start(bf16[64,4096]{1,0:T(8,128)(2,1)} %param.17) | copy-start | bytes 1572868
  7.4 85.9 %all-gather.4.cloned.1.call-start = ((), (), s32[]{:S(2)}) async-start(), calls=%async_computation.2 | async-start | bytes 5242880 | tf_op jit(solution)/shard_map/all_gather | solution.py:23
  8.1 265.9 %reduce-scatter.5.cloned.1.call-start = ((), (), s32[]{:S(2)}) async-start(), calls=%async_computation.3 | async-start | bytes 10485760 | tf_op jit(solution)/shard_map/reduce_scatter | solution.py:31
  93.3 14.7 %copy-start.3 = (bf16[512,4096]{1,0:T(8,128)(2,1)S(1)}, bf16[512,4096]{1,0:T(8,128)(2,1)}, u32[]{:S(2)}) copy-start(bf16[512,4096]{1,0:T(8,128)(2,1)} %all-gather.4.cloned.1.call-done) | copy-start | bytes 12582916
  93.3 27.5 %slice-start = ((s8[14680064]{0:T(1024)(128)(4,1)}), s8[4194304]{0:T(1024)(128)(4,1)S(1)}, s32[]{:S(2)}) async-start(s8[14680064]{0:T(1024)(128)(4,1)} %bitcast.33), calls=%async_computation.8 | async-start | bytes 8388608
  93.3 27.5 %slice-start.1 = ((s8[14680064]{0:T(1024)(128)(4,1)}), s8[4194304]{0:T(1024)(128)(4,1)S(1)}, s32[]{:S(2)}) async-start(s8[14680064]{0:T(1024)(128)(4,1)} %bitcast.33), calls=%async_computation.9 | async-start | bytes 8388608
  107.9 12.9 %slice-start.2 = ((s8[14680064]{0:T(1024)(128)(4,1)}), s8[4194304]{0:T(1024)(128)(4,1)S(1)}, s32[]{:S(2)}) async-start(s8[14680064]{0:T(1024)(128)(4,1)} %bitcast.33), calls=%async_computation.10 | async-start | bytes 8388608
  107.9 12.9 %slice-start.3 = ((s8[14680064]{0:T(1024)(128)(4,1)}), s8[2097152]{0:T(1024)(128)(4,1)S(1)}, s32[]{:S(2)}) async-start(s8[14680064]{0:T(1024)(128)(4,1)} %bitcast.33), calls=%async_computation.11 | async-start | bytes 4194304
  130.8 0.7 copy-start.2
  130.8 143.2 %copy-start.1 = (bf16[4,128,1024]{2,1,0:T(8,128)(2,1)S(1)}, bf16[4,128,1024]{2,1,0:T(8,128)(2,1)}, u32[]{:S(2)}) copy-start(bf16[4,128,1024]{2,1,0:T(8,128)(2,1)} %param.11) | copy-start | bytes 3145732
  130.8 182.5 %all-reduce.2.cloned.1.call-start = ((), (), s32[]{:S(2)}) async-start(), calls=%async_computation.4 | async-start | bytes 524288 | tf_op jit(solution)/shard_map/psum | solution.py:39
  277.1 61.0 %all-gather.6.cloned.1.call-start = ((), (), s32[]{:S(2)}) async-start(), calls=%async_computation.5 | async-start | bytes 10485760 | tf_op jit(solution)/shard_map/all_gather | solution.py:46
  277.7 120.1 %all-gather.8.cloned.1.call-start = ((), (), s32[]{:S(2)}) async-start(), calls=%async_computation.6 | async-start | bytes 10485760 | tf_op jit(solution)/shard_map/all_gather | solution.py:51
  278.3 174.1 %reduce-scatter.7.cloned.1.call-start = ((), (), s32[]{:S(2)}) async-start(), calls=%async_computation.7 | async-start | bytes 2621440
Sparse Core Ops, SparseCore 0:
  9.8 83.4 all-gather.3
  130.9 143.0 reduce-scatter.4
  277.2 36.0 all-reduce.1
  408.5 43.8 reduce-scatter.6
Sparse Core Ops, SparseCore 1:
  279.2 58.8 all-gather.5
  339.6 58.1 all-gather.7
where the time goes:
time: 462 us; the launch traced here: 461 us
  waiting for transfers between devices  390 us (84%)
  matrix products  50.4 us (11%)
  between operations  14.7 us (3%)
    reduce_scatter x1, waiting for transfers between devices, on_device(): lax.psum_scatter(partial_out, 'tensor', scatter_dimension=1, tiled=True)  141 us
    all_gather x1, waiting for transfers between devices, on_device(): piece = lax.all_gather(flat_tokens, 'tensor', axis=1, tiled=True)  85.1 us
    all_gather x1, waiting for transfers between devices, on_device(): lax.all_gather(test_sketches, 'clip', axis=0, tiled=True)  59.7 us
    unnamed x7, waiting for transfers between devices  45.8 us
    psum x1, waiting for transfers between devices, on_device(): lax.psum(jnp.concatenate([left_part, right_part], axis=1), 'tensor')  34.8 us
    all_gather x1, waiting for transfers between devices, on_device(): lax.all_gather(inv_hessian, 'clip', axis=0, tiled=True)  23.4 us
    dot_general x1, matrix products, on_device(): gate_act = jnp.dot(piece, gate_weight, preferred_element_type=jnp.float32)  14.7 us
    dot_general x1, matrix products, on_device(): up_act = jnp.dot(piece, up_weight, preferred_element_type=jnp.float32)  12.8 us
  transfers between devices with their start and end apart: 6, of which 6 were waited for; matrix products, arithmetic and copies ran while one was open for 1% of the time, Pallas kernels for 0%

commit v1 on v0

--- a/solution.py
+++ b/solution.py
@@ -2,6 +2,19 @@
 import jax.numpy as jnp
 from jax import lax
 from jax.sharding import PartitionSpec as P
+
+
+def ring_gather(array, axis, dim):
+    ways = lax.axis_size(axis)
+    up = [(d, (d + 1) % ways) for d in range(ways)]
+    down = [(d, (d - 1) % ways) for d in range(ways)]
+    earlier, later = ([array], [array])
+    for _ in range(ways // 2):
+        earlier.append(lax.ppermute(earlier[-1], axis, up))
+    for _ in range((ways - 1) // 2):
+        later.append(lax.ppermute(later[-1], axis, down))
+    line = jnp.concatenate([*earlier[::-1], *later[1:]], axis=dim)
+    return jnp.roll(line, (lax.axis_index(axis) - ways // 2) * array.shape[dim], axis=dim)
 
 
 def on_device(
@@ -42,9 +55,7 @@
     sketch = jnp.einsum("cti,ctk->cik", left_full, right_full, precision=lax.Precision.HIGHEST)
     flat_sketch = sketch.reshape(clip_count, proj_size * proj_size).astype(jnp.bfloat16)
     precond = jnp.dot(
-        flat_sketch,
-        lax.all_gather(inv_hessian, "clip", axis=0, tiled=True),
-        preferred_element_type=jnp.float32,
+        flat_sketch, ring_gather(inv_hessian, "clip", 0), preferred_element_type=jnp.float32
     ).astype(jnp.bfloat16)
     partial_scores = lax.dot_general(
         precond,

time: 462 us -> 481 us (1.041)
  local copies, waits for them, and re-layouts: 3.53 us -> 25.4 us
    ppermute x0 -> x3, waiting for transfers between devices: none -> 112 us  [the longest x2 112 us: ring_gather(): earlier.append(lax.ppermute(earlier[-1], axis, up))]
    all_gather x1, waiting for transfers between devices: 59.7 us -> 0.03 us  [on_device(): lax.all_gather(test_sketches, 'clip', axis=0, tiled=True)]
    psum x1, waiting for transfers between devices: 34.8 us -> 0.01 us  [on_device(): lax.psum(jnp.concatenate([left_part, right_part], axis=1), 'tensor')]
    all_gather x1 -> x0, waiting for transfers between devices: 23.4 us -> none  [on_device(): lax.all_gather(inv_hessian, 'clip', axis=0, tiled=True)]
    unnamed x18 -> x27, local copies, waits for them, and re-layouts: 3.42 us -> 22.2 us
    unnamed x7 -> x6, waiting for transfers between devices: 45.8 us -> 47.3 us
  transfers between devices with their start and end apart: 6 -> 8, of which waited for: 6 -> 5; matrix products, arithmetic and copies ran while one was open for 1% -> 5% of each run, Pallas kernels for 0% -> 0%
where the time goes in v1:
time: 481 us
  waiting for transfers between devices  386 us (80%)
  matrix products  49.6 us (10%)
  local copies, waits for them, and re-layouts  25.4 us (5%)
  between operations  14.7 us (3%)
    reduce_scatter x1, waiting for transfers between devices, on_device(): lax.psum_scatter(partial_out, 'tensor', scatter_dimension=1, tiled=True)  142 us
    ppermute x2, waiting for transfers between devices, ring_gather(): earlier.append(lax.ppermute(earlier[-1], axis, up))  112 us
    all_gather x1, waiting for transfers between devices, on_device(): piece = lax.all_gather(flat_tokens, 'tensor', axis=1, tiled=True)  85.1 us
    unnamed x6, waiting for transfers between devices  47.3 us
    unnamed x27, local copies, waits for them, and re-layouts  22.2 us
    dot_general x1, matrix products, on_device(): gate_act = jnp.dot(piece, gate_weight, preferred_element_type=jnp.float32)  14.7 us
    dot_general x1, matrix products, on_device(): up_act = jnp.dot(piece, up_weight, preferred_element_type=jnp.float32)  12.8 us
    unnamed x1, matrix products  10.7 us
  transfers between devices with their start and end apart: 8, of which 5 were waited for; matrix products, arithmetic and copies ran while one was open for 5% of the time, Pallas kernels for 0%

profile of v1, /device:TPU:0, one launch (start us, length us, event | category | flops | bytes accessed | tf_op | source)
XLA Modules:
  0.0 481.0 jit_solution(9944647733755991728)
XLA Ops:
  7.4 0.7 all-gather.3.cloned.1.call-update
  8.1 85.1 %all-gather.3.cloned.1.call-done = bf16[512,4096]{1,0:T(8,128)(2,1)} async-done(((bf16[512,1024]{1,0:T(8,128)(2,1)}), bf16[512,4096]{1,0:T(8,128)(2,1)}) %all-gather.3.cloned.1.call-update) | async-done | bytes 4194320 | tf_op jit(solution)/shard_map/all_gather | solution.py:36
  93.3 14.7 %fusion.19 = f32[512,1792]{1,0:T(8,128)} fusion(bf16[512,4096]{1,0:T(8,128)(2,1)} %all-gather.3.cloned.1.call-done, bf16[4096,1792]{1,0:T(8,128)(2,1)} %param.13), kind=kOutput, calls=%fused_computation.31 | convolution fusion | flops 7516192768 | bytes 22544384 | tf_op jit(solution)/shard_map/dot_general | solution.py:37
  108.0 12.8 %multiply_convert_fusion = bf16[512,1792]{1,0:T(8,128)(2,1)S(1)} fusion(f32[512,1792]{1,0:T(8,128)} %fusion.19, bf16[512,4096]{1,0:T(8,128)(2,1)S(1)} %copy-done.4, bf16[4096,1792]{1,0:T(8,128)(2,1)} %param.14), kind=kOutput, calls=%fused_computation.3 | convolution fusion | flops 7521697792 | bytes 24379392 | tf_op jit(solution)/shard_map/dot_general | solution.py:38
  120.8 10.0 %fusion.21 = f32[512,4096]{1,0:T(8,128)} fusion(bf16[512,1792]{1,0:T(8,128)(2,1)S(1)} %multiply_convert_fusion, bf16[1792,4096]{1,0:T(8,128)(2,1)S(1)} %bitcast.33), kind=kOutput, calls=%fused_computation.33 | convolution fusion | flops 7516192768 | bytes 24903680 | tf_op jit(solution)/shard_map/dot_general | solution.py:43
  130.9 0.6 copy-done.3
  131.5 0.1 divide_bitcast_fusion
  131.5 0.2 copy-done.2
  131.8 0.7 fusion.20
  132.4 141.5 %reduce-scatter.5.cloned.1.call-done = f32[512,1024]{1,0:T(8,128)} async-done(((f32[512,4096]{1,0:T(8,128)}), f32[512,1024]{1,0:T(8,128)}) %reduce-scatter.5.cloned.1.call-update) | async-done | bytes 2097168 | tf_op jit(solution)/shard_map/reduce_scatter | solution.py:44
  274.0 2.2 fusion.4
  276.2 0.4 fusion.14
  276.6 0.7 pad_maximum_fusion
  277.4 0.5 all-gather.5.cloned.1.call-update
  278.1 49.0 %collective-permute-done = bf16[1024,1024]{1,0:T(8,128)(2,1)} collective-permute-done((bf16[1024,1024]{1,0:T(8,128)(2,1)S(1)}, bf16[1024,1024]{1,0:T(8,128)(2,1)}, u32[]{:S(2)}, u32[]{:S(2)}) %collective-permute-start) | collective-permute-done | bytes 2097184 | tf_op jit(solution)/shard_map/ppermute | solution.py:13
  327.1 1.3 collective-permute-start.1
  328.4 0.4 collective-permute-start.2
  328.9 63.4 %collective-permute-done.1 = bf16[1024,1024]{1,0:T(8,128)(2,1)} collective-permute-done((bf16[1024,1024]{1,0:T(8,128)(2,1)}, bf16[1024,1024]{1,0:T(8,128)(2,1)}, u32[]{:S(2)}, u32[]{:S(2)}) %collective-permute-start.1) | collective-permute-done | bytes 2097184 | tf_op jit(solution)/shard_map/ppermute | solution.py:13
  392.2 3.1 constant_dynamic-update-slice_fusion.7
  395.3 3.1 constant_dynamic-update-slice_fusion.6
  398.4 1.5 constant_dynamic-update-slice_fusion.5
  399.9 3.1 constant_dynamic-update-slice_fusion.4
  403.0 3.2 constant_dynamic-update-slice_fusion.3
  406.2 3.1 constant_dynamic-update-slice_fusion.2
  409.3 1.5 constant_dynamic-update-slice_fusion.1
  410.8 3.1 constant_dynamic-update-slice_fusion
  413.8 1.0 slice_bitcast_fusion.1
  414.8 0.3 convolution_convert_fusion
  415.2 0.1 convert_element_type.39
  415.3 10.7 %convolution_bitcast_fusion = f32[4096,4]{1,0:T(8,128)} fusion(bf16[4096,1024]{1,0:T(8,128)(2,1)} %all-gather.5.cloned.1.call-done, bf16[4,4096]{1,0:T(4,128)(2,1)S(1)} %convert_element_type.39, bf16[8192,1024]{1,0:T(8,128)(2,1)} %constant_dynamic-update-slice_fusion, s32[]{:T(128)S(6)} %select_n.18), kind=kOutput, calls=%fused_computation.2 | convolution fusion | flops 67112960 | bytes 16875524
  426.0 46.0 %reduce-scatter.7.cloned.1.call-done = f32[1024,4]{1,0:T(8,128)} async-done(((f32[4096,4]{1,0:T(8,128)}), f32[1024,4]{1,0:T(8,128)}) %reduce-scatter.7.cloned.1.call-update) | async-done | bytes 16400
  472.1 1.8 copy.16
  (30 shorter events, 0.3 us)
Async XLA Ops:
  7.4 268.8 %copy-start = (bf16[64,4096]{1,0:T(8,128)(2,1)S(1)}, bf16[64,4096]{1,0:T(8,128)(2,1)}, u32[]{:S(2)}) copy-start(bf16[64,4096]{1,0:T(8,128)(2,1)} %param.17) | copy-start | bytes 1572868
  7.4 85.9 %all-gather.3.cloned.1.call-start = ((), (), s32[]{:S(2)}) async-start(), calls=%async_computation.2 | async-start | bytes 5242880 | tf_op jit(solution)/shard_map/all_gather | solution.py:36
  8.1 265.9 %reduce-scatter.5.cloned.1.call-start = ((), (), s32[]{:S(2)}) async-start(), calls=%async_computation.3 | async-start | bytes 10485760 | tf_op jit(solution)/shard_map/reduce_scatter | solution.py:44
  93.3 14.7 %copy-start.4 = (bf16[512,4096]{1,0:T(8,128)(2,1)S(1)}, bf16[512,4096]{1,0:T(8,128)(2,1)}, u32[]{:S(2)}) copy-start(bf16[512,4096]{1,0:T(8,128)(2,1)} %all-gather.3.cloned.1.call-done) | copy-start | bytes 12582916
  93.3 27.5 %slice-start = ((s8[14680064]{0:T(1024)(128)(4,1)}), s8[4194304]{0:T(1024)(128)(4,1)S(1)}, s32[]{:S(2)}) async-start(s8[14680064]{0:T(1024)(128)(4,1)} %bitcast.32), calls=%async_computation.7 | async-start | bytes 8388608
  93.3 27.5 %slice-start.1 = ((s8[14680064]{0:T(1024)(128)(4,1)}), s8[4194304]{0:T(1024)(128)(4,1)S(1)}, s32[]{:S(2)}) async-start(s8[14680064]{0:T(1024)(128)(4,1)} %bitcast.32), calls=%async_computation.8 | async-start | bytes 8388608
  108.0 12.9 %slice-start.2 = ((s8[14680064]{0:T(1024)(128)(4,1)}), s8[4194304]{0:T(1024)(128)(4,1)S(1)}, s32[]{:S(2)}) async-start(s8[14680064]{0:T(1024)(128)(4,1)} %bitcast.32), calls=%async_computation.9 | async-start | bytes 8388608
  108.0 12.9 %slice-start.3 = ((s8[14680064]{0:T(1024)(128)(4,1)}), s8[2097152]{0:T(1024)(128)(4,1)S(1)}, s32[]{:S(2)}) async-start(s8[14680064]{0:T(1024)(128)(4,1)} %bitcast.32), calls=%async_computation.10 | async-start | bytes 4194304
  130.8 0.7 copy-start.3
  130.8 1.0 copy-start.2
  130.8 283.0 %all-reduce.2.cloned.1.call-start = ((), (), s32[]{:S(2)}) async-start(), calls=%async_computation.4 | async-start | bytes 524288 | tf_op jit(solution)/shard_map/psum | solution.py:52
  132.4 145.6 %copy-start.1 = (bf16[1024,1024]{1,0:T(8,128)(2,1)S(1)}, bf16[1024,1024]{1,0:T(8,128)(2,1)}, u32[]{:S(2)}) copy-start(bf16[1024,1024]{1,0:T(8,128)(2,1)} %param.18) | copy-start | bytes 6291460
  277.4 138.0 %all-gather.5.cloned.1.call-start = ((), (), s32[]{:S(2)}) async-start(), calls=%async_computation.5 | async-start | bytes 10485760 | tf_op jit(solution)/shard_map/all_gather | solution.py:62
  277.9 194.1 %reduce-scatter.7.cloned.1.call-start = ((), (), s32[]{:S(2)}) async-start(), calls=%async_computation.6 | async-start | bytes 2621440
  278.0 49.1 %collective-permute-start = (bf16[1024,1024]{1,0:T(8,128)(2,1)S(1)}, bf16[1024,1024]{1,0:T(8,128)(2,1)}, u32[]{:S(2)}, u32[]{:S(2)}) collective-permute-start(bf16[1024,1024]{1,0:T(8,128)(2,1)S(1)} %copy-done.1), channel_id=1, source_target_pairs={{0,4},{4,8},{8,12},{12,0},{1,5},{5,9},{9,13},{13,1},{2,6},{6,10},{... | collective-permute-start | bytes 6291464 | tf_op jit(solution)/shard_map/ppermute | solution.py:13
  327.1 65.1 %collective-permute-start.1 = (bf16[1024,1024]{1,0:T(8,128)(2,1)}, bf16[1024,1024]{1,0:T(8,128)(2,1)}, u32[]{:S(2)}, u32[]{:S(2)}) collective-permute-start(bf16[1024,1024]{1,0:T(8,128)(2,1)} %collective-permute-done), channel_id=1, source_target_pairs={{0,4},{4,8},{8,12},{12,0},{1,5},{5,9},{9,13},{13,1},{2,6},{6,10},{... | collective-permute-start | bytes 6291464 | tf_op jit(solution)/shard_map/ppermute | solution.py:13
  328.4 71.4 %collective-permute-start.2 = (bf16[1024,1024]{1,0:T(8,128)(2,1)S(1)}, bf16[1024,1024]{1,0:T(8,128)(2,1)}, u32[]{:S(2)}, u32[]{:S(2)}) collective-permute-start(bf16[1024,1024]{1,0:T(8,128)(2,1)S(1)} %copy-done.1), channel_id=1, source_target_pairs={{0,12},{4,0},{8,4},{12,8},{1,13},{5,1},{9,5},{13,9},{2,14},{6,2},{... | collective-permute-start | bytes 6291464 | tf_op jit(solution)/shard_map/ppermute | solution.py:15
Sparse Core Ops, SparseCore 0:
  9.8 83.4 all-gather.2
  131.0 142.9 reduce-scatter.4
  277.5 36.0 all-reduce.1
  426.1 45.8 reduce-scatter.6
Sparse Core Ops, SparseCore 1:
  279.5 87.6 all-gather.4
